TPU v7x, 512 devices: a whole 4x4x16 slice. The times are simulated.
512 devices in a mesh: lon: 64 (over z, x), lat: 8 (over y, core).
Axes of the slice: x: 4, y: 4, z: 16, core: 2. Of those that a mesh axis runs over, the one named last changes fastest.
Arguments:
- wet_mask: int32 [4096, 8192], P('lat', 'lon'), may hold values 0 or 1
- east_level: int32 [4096, 8192], P('lat', 'lon'), may hold values from 0 to 8
- north_level: int32 [4096, 8192], P('lat', 'lon'), may hold values from 0 to 8, as said below
- courant: float32 [4096, 8192], P('lat', 'lon'), may hold values from 0.1 to 0.45
- increment: float32 [4096, 8192], P('lat', 'lon'), may hold values from -6 to 6
- innovation: float32 [4096, 8192], P('lat', 'lon'), may hold values from -6 to 6
- obs_weight: float32 [4096, 8192], P('lat', 'lon'), may hold values from 0.2 to 2
- smooth_scale: float32 [4096], P('lat'), may hold values from 2.5 to 10
Outputs:
- final_eta: float32 [4096, 8192], P('lat', 'lon')
- precond_grad: float32 [4096, 8192], P('lat', 'lon')
Inputs may be any that keep to these rules, and one draw needn't show every extreme that they name: `north_level`: on the top row every north face is open at least half of 8 levels.
All inputs are finite; a program needn't handle non-finite values. No bound on the sum of `wet_mask` on one device may be relied on, other than what follows from the above.
Results may differ from a plain program's by a relative error of at most 0.00023.
Values sent between devices are 32-bit elements; how exact they have to be, the bound alone decides.
A program may use at most 64 MiB of HBM per device.

v0:
```python
import jax
import jax.numpy as jnp
from jax import lax
from jax.sharding import PartitionSpec as P

SUBSTEPS = 4
WLEV = 8


def with_halo(block, sides, width):
    for axis, dim in sides:
        count = lax.axis_size(axis)
        forward = [(i, i + 1) for i in range(count - 1)]
        forward.append((count - 1, 0))
        backward = [(target, source) for source, target in forward]
        low = lax.ppermute(
            lax.slice_in_dim(block, block.shape[dim] - width, None, axis=dim), axis, forward
        )
        high = lax.ppermute(lax.slice_in_dim(block, 0, width, axis=dim), axis, backward)
        block = jnp.concatenate([low, block, high], axis=dim)
    return block


def shifted(value, axis, steps):
    count = lax.axis_size(axis)
    pairs = [(source, (source + steps) % count) for source in range(count)]
    return lax.ppermute(value, axis, pairs)


def passed_along(value, axis, steps):
    count = lax.axis_size(axis)
    leading, last = (max(0, -steps), min(count, count - steps))
    return lax.ppermute(value, axis, [(source, source + steps) for source in range(leading, last)])


def shift_cols(values, stride, eastward):
    if eastward:
        return jnp.pad(values[..., :-stride], ((0, 0), (0, 0), (stride, 0)))
    return jnp.pad(values[..., stride:], ((0, 0), (0, 0), (0, stride)))


def block_cycle(east_end, west_end, block_decay):
    east_sum = east_end
    west_sum = west_end
    weight = block_decay
    blocks_all = east_end.shape[1]
    for bit_index in range(blocks_all.bit_length() - 1):
        stride = 2**bit_index
        east_sum = east_sum + weight * jnp.roll(east_sum, stride, axis=1)
        west_sum = west_sum + weight * jnp.roll(west_sum, -stride, axis=1)
        weight = weight * weight
    return (east_sum, west_sum, blocks_all)


def zonal_solve(source, stiffness, cycle):
    width = source.shape[-1]
    stiff_rows = stiffness[:, None, None]
    root_term = jnp.sqrt(1.0 + 4.0 * stiff_rows)
    log_root = jnp.log1p(-(root_term - 1.0) / (2.0 * stiff_rows))
    green_scale = 1.0 / root_term
    forward_sum = source
    backward_sum = source
    stride = 1
    while stride < width:
        factor = jnp.exp(float(stride) * log_root)
        forward_sum = forward_sum + factor * shift_cols(forward_sum, stride, True)
        backward_sum = backward_sum + factor * shift_cols(backward_sum, stride, False)
        stride = stride * 2
    row_log = log_root[..., 0]
    block_decay = jnp.exp(float(width) * row_log)
    east_end = forward_sum[..., -1]
    west_end = backward_sum[..., 0]
    east_sum, west_sum, blocks_all = cycle(east_end, west_end, block_decay)
    wrap_weight = jnp.exp(float((blocks_all - 1) * width) * row_log)
    image_sum = 1.0 - jnp.exp(float(blocks_all * width) * row_log)
    east_in = ((east_sum - east_end) / block_decay + wrap_weight * east_end) / image_sum
    west_in = ((west_sum - west_end) / block_decay + wrap_weight * west_end) / image_sum
    column = jnp.arange(width, dtype=jnp.float32)
    forward_all = forward_sum + jnp.exp((column + 1.0) * log_root) * east_in[..., None]
    backward_all = backward_sum + jnp.exp((float(width) - column) * log_root) * west_in[..., None]
    return green_scale * (forward_all + backward_all - source)


def mirror_row(values, col_count):
    gathered = lax.all_gather(values, "lon", axis=0, tiled=True)
    return lax.dynamic_slice_in_dim(gathered[::-1], lax.axis_index("lon") * col_count, col_count)


def laplace(state_now, face_set, at_top):
    east_face, west_face, north_face, south_face = face_set
    padded = with_halo(state_now, (("lat", 0), ("lon", 1)), 1)
    folded = mirror_row(state_now[-1], state_now.shape[1])
    north_vals = padded[2:, 1:-1]
    north_vals = north_vals.at[-1].set(jnp.where(at_top, folded, north_vals[-1]))
    return (
        east_face * (padded[1:-1, 2:] - state_now)
        + west_face * (padded[1:-1, :-2] - state_now)
        + north_face * (north_vals - state_now)
        + south_face * (padded[:-2, 1:-1] - state_now)
    )


def local(
    wet_mask, east_level, north_level, courant, increment, innovation, obs_weight, smooth_scale
):
    row_count, col_count = increment.shape
    lon_count = lax.axis_size("lon")
    at_top = lax.axis_index("lat") == lax.axis_size("lat") - 1
    wet_frac = wet_mask.astype(jnp.float32)
    east_face = east_level.astype(jnp.float32) / WLEV
    raw_north = north_level.astype(jnp.float32) / WLEV
    west_edge = shifted(east_face[:, -1], "lon", 1)
    west_face = jnp.concatenate([west_edge[:, None], east_face[:, :-1]], axis=1)
    south_edge = passed_along(raw_north[-1], "lat", 1)
    south_face = jnp.concatenate([south_edge[None], raw_north[:-1]], axis=0)
    top_faces = raw_north[-1]
    fold_face = top_faces * mirror_row(top_faces, col_count)
    north_face = raw_north.at[-1].set(jnp.where(at_top, fold_face, top_faces))
    face_set = (east_face, west_face, north_face, south_face)
    state_now = wet_frac * increment
    before = state_now
    for substep in range(SUBSTEPS):
        after = 2.0 * state_now - before + wet_frac * courant * laplace(state_now, face_set, at_top)
        before = state_now
        state_now = after
    adjoint = wet_frac * obs_weight * (state_now - innovation)
    carried = jnp.zeros_like(adjoint)
    for substep in range(SUBSTEPS):
        updated = (
            2.0 * adjoint
            + wet_frac * laplace(courant * wet_frac * adjoint, face_set, at_top)
            + carried
        )
        carried = -adjoint
        adjoint = updated
    gradient = wet_frac * (adjoint + carried)
    lines = lax.all_to_all(gradient, "lon", split_axis=0, concat_axis=1, tiled=True)
    line_rows = row_count // lon_count
    row_scales = lax.dynamic_slice_in_dim(
        smooth_scale, lax.axis_index("lon") * line_rows, line_rows
    )
    stiffness = row_scales * float(col_count * col_count)
    blocked = lines.reshape(line_rows, lon_count, col_count)
    smoothed = zonal_solve(blocked, stiffness, block_cycle).reshape(
        line_rows, lon_count * col_count
    )
    smoothed = smoothed * (2.0 * stiffness**0.25)[:, None]
    precond_grad = lax.all_to_all(smoothed, "lon", split_axis=1, concat_axis=0, tiled=True)
    return (state_now, precond_grad)


def solution(mesh):
    return jax.shard_map(
        local,
        mesh=mesh,
        in_specs=(
            P("lat", "lon"),
            P("lat", "lon"),
            P("lat", "lon"),
            P("lat", "lon"),
            P("lat", "lon"),
            P("lat", "lon"),
            P("lat", "lon"),
            P("lat"),
        ),
        out_specs=(P("lat", "lon"), P("lat", "lon")),
        check_vma=False,
    )
```

profile of v0, /device:TPU:2, one launch (start us, length us, event | category | flops | bytes accessed | tf_op | source)
XLA Modules:
  0.0 885.1 jit_solution(8038742436026527924)
XLA Ops:
  0.6 1.1 convert_multiply_fusion.3
  1.8 2.9 collective-permute-start.1
  4.8 1.3 collective-permute-start.5
  6.3 3.4 collective-permute-start.3
  9.7 79.2 %all-gather = f32[1,8192]{1,0:T(1,128)S(1)} all-gather(f32[1,128]{1,0:T(1,128)S(1)} %get-tuple-element.160), channel_id=2, replica_groups=mesh['lon'=64,'lat'=8] {'lon'}, dimensions={1}, use_global_device_ids=true | all-gather | bytes 33280 | tf_op jit(solution)/shard_map/all_gather | solution.py:85
  89.1 72.9 %all-gather.1 = f32[1,8192]{1,0:T(1,128)S(1)} all-gather(f32[1,128]{1,0:T(1,128)S(1)} %get-tuple-element.162), channel_id=3, replica_groups=mesh['lon'=64,'lat'=8] {'lon'}, dimensions={1}, use_global_device_ids=true | all-gather | bytes 33280 | tf_op jit(solution)/shard_map/all_gather | solution.py:85
  163.0 2.9 collective-permute-start.4
  165.9 2.9 collective-permute-start.2
  169.2 2.3 collective-permute-done.4
  171.5 2.7 collective-permute-done.2
  174.2 1.4 fusion
  175.6 2.9 collective-permute-start.7
  178.5 75.9 %all-gather.2 = f32[1,8192]{1,0:T(1,128)S(1)} all-gather(f32[1,128]{1,0:T(1,128)S(1)} %get-tuple-element.158), channel_id=4, replica_groups=mesh['lon'=64,'lat'=8] {'lon'}, dimensions={1}, use_global_device_ids=true | all-gather | bytes 33280 | tf_op jit(solution)/shard_map/all_gather | solution.py:85
  255.4 2.0 collective-permute-start.9
  257.4 3.9 collective-permute-start.8
  261.4 2.5 collective-permute-done.9
  263.9 1.8 collective-permute-done.8
  266.1 2.9 collective-permute-start.11
  269.0 75.5 %all-gather.3 = f32[1,8192]{1,0:T(1,128)S(1)} all-gather(f32[1,128]{1,0:T(1,128)S(1)} %get-tuple-element.156), channel_id=5, replica_groups=mesh['lon'=64,'lat'=8] {'lon'}, dimensions={1}, use_global_device_ids=true | all-gather | bytes 33280 | tf_op jit(solution)/shard_map/all_gather | solution.py:85
  345.5 3.0 collective-permute-start.13
  348.5 2.9 collective-permute-start.12
  351.5 2.5 collective-permute-done.13
  354.1 2.8 collective-permute-done.12
  357.2 2.9 collective-permute-start.15
  360.2 75.6 %all-gather.4 = f32[1,8192]{1,0:T(1,128)S(1)} all-gather(f32[1,128]{1,0:T(1,128)S(1)} %get-tuple-element.154), channel_id=6, replica_groups=mesh['lon'=64,'lat'=8] {'lon'}, dimensions={1}, use_global_device_ids=true | all-gather | bytes 33280 | tf_op jit(solution)/shard_map/all_gather | solution.py:85
  435.8 0.9 fusion.149
  436.7 2.0 collective-permute-start.17
  438.7 3.9 collective-permute-start.16
  442.7 2.5 collective-permute-done.17
  445.2 2.0 collective-permute-done.16
  447.2 2.1 fusion.142
  449.3 3.0 collective-permute-start.19
  452.3 76.7 %all-gather.5 = f32[1,8192]{1,0:T(1,128)S(1)} all-gather(f32[1,128]{1,0:T(1,128)S(1)} %get-tuple-element.152), channel_id=7, replica_groups=mesh['lon'=64,'lat'=8] {'lon'}, dimensions={1}, use_global_device_ids=true | all-gather | bytes 33280 | tf_op jit(solution)/shard_map/all_gather | solution.py:85
  529.2 3.0 collective-permute-start.21
  532.2 2.9 collective-permute-start.20
  535.2 2.3 collective-permute-done.21
  537.5 3.1 collective-permute-done.20
  540.6 1.3 fusion.140
  542.0 2.9 collective-permute-start.23
  544.9 75.6 %all-gather.6 = f32[1,8192]{1,0:T(1,128)S(1)} all-gather(f32[1,128]{1,0:T(1,128)S(1)} %get-tuple-element.150), channel_id=8, replica_groups=mesh['lon'=64,'lat'=8] {'lon'}, dimensions={1}, use_global_device_ids=true | all-gather | bytes 33280 | tf_op jit(solution)/shard_map/all_gather | solution.py:85
  620.6 0.9 fusion.147
  621.5 2.0 collective-permute-start.25
  623.4 3.9 collective-permute-start.24
  627.5 2.5 collective-permute-done.25
  630.0 2.1 collective-permute-done.24
  632.1 1.3 fusion.138
  633.5 2.9 collective-permute-start.27
  636.4 75.5 %all-gather.7 = f32[1,8192]{1,0:T(1,128)S(1)} all-gather(f32[1,128]{1,0:T(1,128)S(1)} %get-tuple-element.148), channel_id=9, replica_groups=mesh['lon'=64,'lat'=8] {'lon'}, dimensions={1}, use_global_device_ids=true | all-gather | bytes 33280 | tf_op jit(solution)/shard_map/all_gather | solution.py:85
  712.1 0.9 fusion.146
  712.9 3.0 collective-permute-start.29
  715.9 2.9 collective-permute-start.28
  718.9 2.5 collective-permute-done.29
  721.4 3.1 collective-permute-done.28
  724.5 1.3 fusion.136
  725.9 2.9 collective-permute-start.31
  728.8 75.6 %all-gather.8 = f32[1,8192]{1,0:T(1,128)S(1)} all-gather(f32[1,128]{1,0:T(1,128)S(1)} %get-tuple-element.146), channel_id=10, replica_groups=mesh['lon'=64,'lat'=8] {'lon'}, dimensions={1}, use_global_device_ids=true | all-gather | bytes 33280 | tf_op jit(solution)/shard_map/all_gather | solution.py:85
  805.4 2.0 collective-permute-start.33
  807.3 3.9 collective-permute-start.32
  811.4 2.8 collective-permute-done.33
  814.2 1.8 collective-permute-done.32
  816.0 1.1 fusion.9
  817.0 17.4 %all-to-all-start = ((f32[64,8,128]{2,1,0:T(8,128)}), f32[64,8,128]{2,1,0:T(8,128)S(1)}, u32[]{:S(2)}, u32[]{:S(2)}) async-start(f32[64,8,128]{2,1,0:T(8,128)} %fusion.9), calls=%async_computation | async-start | bytes 524288 | tf_op jit(solution)/shard_map/all_to_all | solution.py:137
  835.4 21.2 %all-to-all-done = f32[64,8,128]{2,1,0:T(8,128)S(1)} async-done(((f32[64,8,128]{2,1,0:T(8,128)}), f32[64,8,128]{2,1,0:T(8,128)S(1)}, u32[]{:S(2)}, u32[]{:S(2)}) %all-to-all-start) | async-done | bytes 262176 | tf_op jit(solution)/shard_map/all_to_all | solution.py:137
  860.6 23.8 %all_to_all.32 = f32[8,64,128]{2,0,1:T(8,128)S(1)} all-to-all(f32[8,64,128]{2,0,1:T(8,128)S(1)} %copy.746), channel_id=1, replica_groups=mesh['lon'=64,'lat'=8] {'lon'}, dimensions={1} | all-to-all | bytes 524288 | tf_op jit(solution)/shard_map/all_to_all | solution.py:148
  (155 shorter events, 12.6 us)
Async XLA Ops:
  0.6 4.1 copy-start.2
  1.8 160.3 %collective-permute-start = (f32[1,128]{1,0:T(1,128)S(1)}, f32[1,128]{1,0:T(1,128)S(1)}, u32[]{:S(2)}, u32[]{:S(2)}) collective-permute-start(f32[1,128]{1,0:T(1,128)S(1)} %get-tuple-element.162), channel_id=1, source_target_pairs={{0,1},{1,2},{2,3},{3,4},{4,5},{5,6},{6,7},{7,0},{8,9},{9,10},{10,1... | collective-permute-start | bytes 1544 | tf_op jit(solution)/shard_map/ppermute | solution.py:16
  1.8 4.3 copy-start
  1.8 160.3 %collective-permute-start.1 = (f32[1,128]{1,0:T(1,128)S(1)}, f32[1,128]{1,0:T(1,128)S(1)}, u32[]{:S(2)}, u32[]{:S(2)}) collective-permute-start(f32[1,128]{1,0:T(1,128)S(1)} %get-tuple-element.161), channel_id=1, source_target_pairs={{1,0},{2,1},{3,2},{4,3},{5,4},{6,5},{7,6},{0,7},{9,8},{10,9},{11,1... | collective-permute-start | bytes 1544 | tf_op jit(solution)/shard_map/ppermute | solution.py:19
  4.8 164.4 %collective-permute-start.5 = (f32[128]{0:T(128)S(1)}, f32[128]{0:T(128)S(1)}, u32[]{:S(2)}, u32[]{:S(2)}) collective-permute-start(f32[128]{0:T(128)S(1)} %get-tuple-element.159), channel_id=1, source_target_pairs={{0,1},{1,2},{2,3},{3,4},{4,5},{5,6},{6,7},{8,9},{9,10},{10,11},{11... | collective-permute-start | bytes 1544 | tf_op jit(solution)/shard_map/ppermute | solution.py:33
  6.3 162.6 %collective-permute-start.3 = (f32[512]{0:T(512)S(1)}, f32[512]{0:T(512)S(1)}, u32[]{:S(2)}, u32[]{:S(2)}) collective-permute-start(f32[512]{0:T(512)S(1)} %slice_reduce_fusion), channel_id=1, source_target_pairs={{0,8},{8,16},{16,24},{24,32},{32,40},{40,48},{48,56},{56,64},{64,7... | collective-permute-start | bytes 6152 | tf_op jit(solution)/shard_map/ppermute | solution.py:27
  163.0 8.5 collective-permute-start.4
  165.9 8.3 collective-permute-start.2
  168.9 5.3 copy-start.1
  175.6 79.0 %collective-permute-start.6 = (f32[1,128]{1,0:T(1,128)S(1)}, f32[1,128]{1,0:T(1,128)S(1)}, u32[]{:S(2)}, u32[]{:S(2)}) collective-permute-start(f32[1,128]{1,0:T(1,128)S(1)} %get-tuple-element.158), channel_id=1, source_target_pairs={{0,1},{1,2},{2,3},{3,4},{4,5},{5,6},{6,7},{7,0},{8,9},{9,10},{10,1... | collective-permute-start | bytes 1544 | tf_op jit(solution)/shard_map/ppermute | solution.py:16
  175.6 78.9 %collective-permute-start.7 = (f32[1,128]{1,0:T(1,128)S(1)}, f32[1,128]{1,0:T(1,128)S(1)}, u32[]{:S(2)}, u32[]{:S(2)}) collective-permute-start(f32[1,128]{1,0:T(1,128)S(1)} %get-tuple-element.157), channel_id=1, source_target_pairs={{1,0},{2,1},{3,2},{4,3},{5,4},{6,5},{7,6},{0,7},{9,8},{10,9},{11,1... | collective-permute-start | bytes 1544 | tf_op jit(solution)/shard_map/ppermute | solution.py:19
  255.4 8.5 collective-permute-start.9
  257.4 8.3 collective-permute-start.8
  266.1 78.6 %collective-permute-start.10 = (f32[1,128]{1,0:T(1,128)S(1)}, f32[1,128]{1,0:T(1,128)S(1)}, u32[]{:S(2)}, u32[]{:S(2)}) collective-permute-start(f32[1,128]{1,0:T(1,128)S(1)} %get-tuple-element.156), channel_id=1, source_target_pairs={{0,1},{1,2},{2,3},{3,4},{4,5},{5,6},{6,7},{7,0},{8,9},{9,10},{10,1... | collective-permute-start | bytes 1544 | tf_op jit(solution)/shard_map/ppermute | solution.py:16
  266.1 78.6 %collective-permute-start.11 = (f32[1,128]{1,0:T(1,128)S(1)}, f32[1,128]{1,0:T(1,128)S(1)}, u32[]{:S(2)}, u32[]{:S(2)}) collective-permute-start(f32[1,128]{1,0:T(1,128)S(1)} %get-tuple-element.155), channel_id=1, source_target_pairs={{1,0},{2,1},{3,2},{4,3},{5,4},{6,5},{7,6},{0,7},{9,8},{10,9},{11,1... | collective-permute-start | bytes 1544 | tf_op jit(solution)/shard_map/ppermute | solution.py:19
  345.5 8.5 collective-permute-start.13
  348.5 8.3 collective-permute-start.12
  357.2 78.6 %collective-permute-start.14 = (f32[1,128]{1,0:T(1,128)S(1)}, f32[1,128]{1,0:T(1,128)S(1)}, u32[]{:S(2)}, u32[]{:S(2)}) collective-permute-start(f32[1,128]{1,0:T(1,128)S(1)} %get-tuple-element.154), channel_id=1, source_target_pairs={{0,1},{1,2},{2,3},{3,4},{4,5},{5,6},{6,7},{7,0},{8,9},{9,10},{10,1... | collective-permute-start | bytes 1544 | tf_op jit(solution)/shard_map/ppermute | solution.py:16
  357.2 78.6 %collective-permute-start.15 = (f32[1,128]{1,0:T(1,128)S(1)}, f32[1,128]{1,0:T(1,128)S(1)}, u32[]{:S(2)}, u32[]{:S(2)}) collective-permute-start(f32[1,128]{1,0:T(1,128)S(1)} %get-tuple-element.153), channel_id=1, source_target_pairs={{1,0},{2,1},{3,2},{4,3},{5,4},{6,5},{7,6},{0,7},{9,8},{10,9},{11,1... | collective-permute-start | bytes 1544 | tf_op jit(solution)/shard_map/ppermute | solution.py:19
  436.7 8.5 collective-permute-start.17
  438.7 8.5 collective-permute-start.16
  449.3 79.8 %collective-permute-start.18 = (f32[1,128]{1,0:T(1,128)S(1)}, f32[1,128]{1,0:T(1,128)S(1)}, u32[]{:S(2)}, u32[]{:S(2)}) collective-permute-start(f32[1,128]{1,0:T(1,128)S(1)} %get-tuple-element.152), channel_id=1, source_target_pairs={{0,1},{1,2},{2,3},{3,4},{4,5},{5,6},{6,7},{7,0},{8,9},{9,10},{10,1... | collective-permute-start | bytes 1544 | tf_op jit(solution)/shard_map/ppermute | solution.py:16
  449.3 79.8 %collective-permute-start.19 = (f32[1,128]{1,0:T(1,128)S(1)}, f32[1,128]{1,0:T(1,128)S(1)}, u32[]{:S(2)}, u32[]{:S(2)}) collective-permute-start(f32[1,128]{1,0:T(1,128)S(1)} %get-tuple-element.151), channel_id=1, source_target_pairs={{1,0},{2,1},{3,2},{4,3},{5,4},{6,5},{7,6},{0,7},{9,8},{10,9},{11,1... | collective-permute-start | bytes 1544 | tf_op jit(solution)/shard_map/ppermute | solution.py:19
  529.2 8.3 collective-permute-start.21
  532.2 8.4 collective-permute-start.20
  541.9 78.6 %collective-permute-start.22 = (f32[1,128]{1,0:T(1,128)S(1)}, f32[1,128]{1,0:T(1,128)S(1)}, u32[]{:S(2)}, u32[]{:S(2)}) collective-permute-start(f32[1,128]{1,0:T(1,128)S(1)} %get-tuple-element.150), channel_id=1, source_target_pairs={{0,1},{1,2},{2,3},{3,4},{4,5},{5,6},{6,7},{7,0},{8,9},{9,10},{10,1... | collective-permute-start | bytes 1544 | tf_op jit(solution)/shard_map/ppermute | solution.py:16
  542.0 78.6 %collective-permute-start.23 = (f32[1,128]{1,0:T(1,128)S(1)}, f32[1,128]{1,0:T(1,128)S(1)}, u32[]{:S(2)}, u32[]{:S(2)}) collective-permute-start(f32[1,128]{1,0:T(1,128)S(1)} %get-tuple-element.149), channel_id=1, source_target_pairs={{1,0},{2,1},{3,2},{4,3},{5,4},{6,5},{7,6},{0,7},{9,8},{10,9},{11,1... | collective-permute-start | bytes 1544 | tf_op jit(solution)/shard_map/ppermute | solution.py:19
  621.5 8.5 collective-permute-start.25
  623.4 8.7 collective-permute-start.24
  633.4 78.6 %collective-permute-start.26 = (f32[1,128]{1,0:T(1,128)S(1)}, f32[1,128]{1,0:T(1,128)S(1)}, u32[]{:S(2)}, u32[]{:S(2)}) collective-permute-start(f32[1,128]{1,0:T(1,128)S(1)} %get-tuple-element.148), channel_id=1, source_target_pairs={{0,1},{1,2},{2,3},{3,4},{4,5},{5,6},{6,7},{7,0},{8,9},{9,10},{10,1... | collective-permute-start | bytes 1544 | tf_op jit(solution)/shard_map/ppermute | solution.py:16
  633.5 78.6 %collective-permute-start.27 = (f32[1,128]{1,0:T(1,128)S(1)}, f32[1,128]{1,0:T(1,128)S(1)}, u32[]{:S(2)}, u32[]{:S(2)}) collective-permute-start(f32[1,128]{1,0:T(1,128)S(1)} %get-tuple-element.147), channel_id=1, source_target_pairs={{1,0},{2,1},{3,2},{4,3},{5,4},{6,5},{7,6},{0,7},{9,8},{10,9},{11,1... | collective-permute-start | bytes 1544 | tf_op jit(solution)/shard_map/ppermute | solution.py:19
  712.9 8.5 collective-permute-start.29
  715.9 8.6 collective-permute-start.28
  725.9 78.6 %collective-permute-start.30 = (f32[1,128]{1,0:T(1,128)S(1)}, f32[1,128]{1,0:T(1,128)S(1)}, u32[]{:S(2)}, u32[]{:S(2)}) collective-permute-start(f32[1,128]{1,0:T(1,128)S(1)} %get-tuple-element.146), channel_id=1, source_target_pairs={{0,1},{1,2},{2,3},{3,4},{4,5},{5,6},{6,7},{7,0},{8,9},{9,10},{10,1... | collective-permute-start | bytes 1544 | tf_op jit(solution)/shard_map/ppermute | solution.py:16
  725.9 78.6 %collective-permute-start.31 = (f32[1,128]{1,0:T(1,128)S(1)}, f32[1,128]{1,0:T(1,128)S(1)}, u32[]{:S(2)}, u32[]{:S(2)}) collective-permute-start(f32[1,128]{1,0:T(1,128)S(1)} %get-tuple-element.145), channel_id=1, source_target_pairs={{1,0},{2,1},{3,2},{4,3},{5,4},{6,5},{7,6},{0,7},{9,8},{10,9},{11,1... | collective-permute-start | bytes 1544 | tf_op jit(solution)/shard_map/ppermute | solution.py:19
  805.4 8.8 collective-permute-start.33
  807.3 8.6 collective-permute-start.32
  817.0 39.5 %all-to-all-start = ((f32[64,8,128]{2,1,0:T(8,128)}), f32[64,8,128]{2,1,0:T(8,128)S(1)}, u32[]{:S(2)}, u32[]{:S(2)}) async-start(f32[64,8,128]{2,1,0:T(8,128)} %fusion.9), calls=%async_computation | async-start | bytes 524288 | tf_op jit(solution)/shard_map/all_to_all | solution.py:137
where the time goes:
time: 886 us; the launch traced here: 885 us
  blocking collectives  706 us (80%)
  starting transfers between devices  92.4 us (10%)
  waiting for transfers between devices  60.6 us (7%)
  other arithmetic  14.4 us (2%)
  local copies, waits for them, and re-layouts  10.2 us (1%)
    all_gather x9, blocking collectives, mirror_row(): gathered = lax.all_gather(values, 'lon', axis=0, tiled=True)  682 us
    ppermute x16, starting transfers between devices, with_halo(): lax.ppermute(lax.slice_in_dim(block, 0, width, axis=dim), axis, backward)  50.6 us
    all_to_all x1, blocking collectives, local(): lax.all_to_all(smoothed, 'lon', split_axis=1, concat_axis=0, tiled=True)  23.8 us
    all_to_all x1, waiting for transfers between devices, local(): lax.all_to_all(gradient, 'lon', split_axis=0, concat_axis=1, tiled=True)  21.2 us
    ppermute x16, waiting for transfers between devices, with_halo(): lax.ppermute(lax.slice_in_dim(block, block.shape[dim] - width, None, axis...  20.1 us
    ppermute x16, starting transfers between devices, with_halo(): lax.ppermute(lax.slice_in_dim(block, block.shape[dim] - width, None, axis...  19.8 us
    ppermute x16, waiting for transfers between devices, with_halo(): lax.ppermute(lax.slice_in_dim(block, 0, width, axis=dim), axis, backward)  19.4 us
  transfers between devices with their start and end apart: 35, of which 17 were waited for; matrix products, arithmetic and copies ran while one was open for 0% of the time, Pallas kernels for 0%

commit v1 on v0

--- a/solution.py
+++ b/solution.py
@@ -134,7 +134,10 @@
         carried = -adjoint
         adjoint = updated
     gradient = wet_frac * (adjoint + carried)
-    lines = lax.all_to_all(gradient, "lon", split_axis=0, concat_axis=1, tiled=True)
+    lines = jnp.concatenate(
+        lax.all_to_all(jnp.stack(jnp.split(gradient, lax.axis_size("lon"), axis=0)), "lon", 0, 0),
+        axis=1,
+    )
     line_rows = row_count // lon_count
     row_scales = lax.dynamic_slice_in_dim(
         smooth_scale, lax.axis_index("lon") * line_rows, line_rows

time: 886 us -> 919 us (1.037)
  local copies, waits for them, and re-layouts: 10.2 us -> 48.1 us
    unnamed x8 -> x71, local copies, waits for them, and re-layouts: 0.74 us -> 38.1 us
where the time goes in v1:
time: 919 us; the launch traced here: 918 us
  blocking collectives  708 us (77%)
  starting transfers between devices  89 us (10%)
  waiting for transfers between devices  57.4 us (6%)
  local copies, waits for them, and re-layouts  48.1 us (5%)
  other arithmetic  13.7 us (1%)
    all_gather x9, blocking collectives, mirror_row(): gathered = lax.all_gather(values, 'lon', axis=0, tiled=True)  682 us
    ppermute x16, starting transfers between devices, with_halo(): lax.ppermute(lax.slice_in_dim(block, 0, width, axis=dim), axis, backward)  50.6 us
    unnamed x71, local copies, waits for them, and re-layouts  38.1 us
    all_to_all x1, blocking collectives, local(): lax.all_to_all(smoothed, 'lon', split_axis=1, concat_axis=0, tiled=True)  25.7 us
    ppermute x16, waiting for transfers between devices, with_halo(): lax.ppermute(lax.slice_in_dim(block, block.shape[dim] - width, None, axis...  19.8 us
    ppermute x16, starting transfers between devices, with_halo(): lax.ppermute(lax.slice_in_dim(block, block.shape[dim] - width, None, axis...  19.8 us
    ppermute x16, waiting for transfers between devices, with_halo(): lax.ppermute(lax.slice_in_dim(block, 0, width, axis=dim), axis, backward)  19.4 us
  transfers between devices with their start and end apart: 35, of which 17 were waited for; matrix products, arithmetic and copies ran while one was open for 0% of the time, Pallas kernels for 0%

profile of v1, /device:TPU:2, one launch (start us, length us, event | category | flops | bytes accessed | tf_op | source)
XLA Modules:
  0.0 917.7 jit_solution(13481285260757724309)
XLA Ops:
  0.6 1.1 convert_multiply_fusion.3
  1.8 2.9 collective-permute-start.1
  4.8 1.3 collective-permute-start.5
  6.3 3.4 collective-permute-start.3
  9.7 79.2 %all-gather = f32[1,8192]{1,0:T(1,128)S(1)} all-gather(f32[1,128]{1,0:T(1,128)S(1)} %get-tuple-element.190), channel_id=2, replica_groups=mesh['lon'=64,'lat'=8] {'lon'}, dimensions={1}, use_global_device_ids=true | all-gather | bytes 33280 | tf_op jit(solution)/shard_map/all_gather | solution.py:85
  89.1 72.9 %all-gather.1 = f32[1,8192]{1,0:T(1,128)S(1)} all-gather(f32[1,128]{1,0:T(1,128)S(1)} %get-tuple-element.192), channel_id=3, replica_groups=mesh['lon'=64,'lat'=8] {'lon'}, dimensions={1}, use_global_device_ids=true | all-gather | bytes 33280 | tf_op jit(solution)/shard_map/all_gather | solution.py:85
  162.1 0.9 fusion.151
  163.0 2.9 collective-permute-start.4
  165.9 2.9 collective-permute-start.2
  169.2 2.3 collective-permute-done.4
  171.5 2.7 collective-permute-done.2
  174.2 1.4 fusion
  175.6 2.9 collective-permute-start.7
  178.5 75.9 %all-gather.2 = f32[1,8192]{1,0:T(1,128)S(1)} all-gather(f32[1,128]{1,0:T(1,128)S(1)} %get-tuple-element.188), channel_id=4, replica_groups=mesh['lon'=64,'lat'=8] {'lon'}, dimensions={1}, use_global_device_ids=true | all-gather | bytes 33280 | tf_op jit(solution)/shard_map/all_gather | solution.py:85
  255.4 2.0 collective-permute-start.9
  257.4 3.9 collective-permute-start.8
  261.4 2.5 collective-permute-done.9
  263.9 1.8 collective-permute-done.8
  266.1 2.9 collective-permute-start.11
  269.0 75.5 %all-gather.3 = f32[1,8192]{1,0:T(1,128)S(1)} all-gather(f32[1,128]{1,0:T(1,128)S(1)} %get-tuple-element.186), channel_id=5, replica_groups=mesh['lon'=64,'lat'=8] {'lon'}, dimensions={1}, use_global_device_ids=true | all-gather | bytes 33280 | tf_op jit(solution)/shard_map/all_gather | solution.py:85
  345.5 3.0 collective-permute-start.13
  348.5 2.9 collective-permute-start.12
  351.5 2.5 collective-permute-done.13
  354.1 2.8 collective-permute-done.12
  357.2 2.9 collective-permute-start.15
  360.2 75.6 %all-gather.4 = f32[1,8192]{1,0:T(1,128)S(1)} all-gather(f32[1,128]{1,0:T(1,128)S(1)} %get-tuple-element.184), channel_id=6, replica_groups=mesh['lon'=64,'lat'=8] {'lon'}, dimensions={1}, use_global_device_ids=true | all-gather | bytes 33280 | tf_op jit(solution)/shard_map/all_gather | solution.py:85
  435.8 0.9 fusion.148
  436.7 2.0 collective-permute-start.17
  438.7 3.9 collective-permute-start.16
  442.7 2.5 collective-permute-done.17
  445.2 2.0 collective-permute-done.16
  447.2 2.1 fusion.141
  449.3 3.0 collective-permute-start.19
  452.3 76.7 %all-gather.5 = f32[1,8192]{1,0:T(1,128)S(1)} all-gather(f32[1,128]{1,0:T(1,128)S(1)} %get-tuple-element.182), channel_id=7, replica_groups=mesh['lon'=64,'lat'=8] {'lon'}, dimensions={1}, use_global_device_ids=true | all-gather | bytes 33280 | tf_op jit(solution)/shard_map/all_gather | solution.py:85
  529.2 3.0 collective-permute-start.21
  532.2 2.9 collective-permute-start.20
  535.2 2.3 collective-permute-done.21
  537.5 3.1 collective-permute-done.20
  540.6 1.3 fusion.139
  542.0 2.9 collective-permute-start.23
  544.9 75.6 %all-gather.6 = f32[1,8192]{1,0:T(1,128)S(1)} all-gather(f32[1,128]{1,0:T(1,128)S(1)} %get-tuple-element.180), channel_id=8, replica_groups=mesh['lon'=64,'lat'=8] {'lon'}, dimensions={1}, use_global_device_ids=true | all-gather | bytes 33280 | tf_op jit(solution)/shard_map/all_gather | solution.py:85
  620.6 0.9 fusion.146
  621.5 2.0 collective-permute-start.25
  623.4 3.9 collective-permute-start.24
  627.5 2.5 collective-permute-done.25
  630.0 2.1 collective-permute-done.24
  632.1 1.3 fusion.137
  633.5 2.9 collective-permute-start.27
  636.4 75.5 %all-gather.7 = f32[1,8192]{1,0:T(1,128)S(1)} all-gather(f32[1,128]{1,0:T(1,128)S(1)} %get-tuple-element.178), channel_id=9, replica_groups=mesh['lon'=64,'lat'=8] {'lon'}, dimensions={1}, use_global_device_ids=true | all-gather | bytes 33280 | tf_op jit(solution)/shard_map/all_gather | solution.py:85
  712.1 0.9 fusion.145
  712.9 3.0 collective-permute-start.29
  715.9 2.9 collective-permute-start.28
  718.9 2.5 collective-permute-done.29
  721.4 3.1 collective-permute-done.28
  724.5 1.3 fusion.135
  725.9 2.9 collective-permute-start.31
  728.8 75.6 %all-gather.8 = f32[1,8192]{1,0:T(1,128)S(1)} all-gather(f32[1,128]{1,0:T(1,128)S(1)} %get-tuple-element.176), channel_id=10, replica_groups=mesh['lon'=64,'lat'=8] {'lon'}, dimensions={1}, use_global_device_ids=true | all-gather | bytes 33280 | tf_op jit(solution)/shard_map/all_gather | solution.py:85
  805.4 2.0 collective-permute-start.33
  807.3 3.9 collective-permute-start.32
  811.4 2.5 collective-permute-done.33
  813.9 1.8 collective-permute-done.32
  854.0 14.0 %all-to-all-start = ((f32[64,8,128]{2,1,0:T(8,128)}), f32[64,8,128]{2,1,0:T(8,128)S(1)}, u32[]{:S(2)}, u32[]{:S(2)}) async-start(f32[64,8,128]{2,1,0:T(8,128)} %constant_dynamic-update-slice_fusion), calls=%async_computation | async-start | bytes 524288 | tf_op jit(solution)/shard_map/all_to_all | solution.py:138
  869.0 18.3 %all-to-all-done = f32[64,8,128]{2,1,0:T(8,128)S(1)} async-done(((f32[64,8,128]{2,1,0:T(8,128)}), f32[64,8,128]{2,1,0:T(8,128)S(1)}, u32[]{:S(2)}, u32[]{:S(2)}) %all-to-all-start) | async-done | bytes 262176 | tf_op jit(solution)/shard_map/all_to_all | solution.py:138
  891.3 25.7 %all_to_all.21 = f32[8,64,128]{2,0,1:T(8,128)S(1)} all-to-all(f32[8,64,128]{2,0,1:T(8,128)S(1)} %copy.2507), channel_id=1, replica_groups=mesh['lon'=64,'lat'=8] {'lon'}, dimensions={1} | all-to-all | bytes 524288 | tf_op jit(solution)/shard_map/all_to_all | solution.py:151
  (219 shorter events, 50.0 us)
Async XLA Ops:
  0.6 4.1 copy-start.2
  1.8 160.3 %collective-permute-start = (f32[1,128]{1,0:T(1,128)S(1)}, f32[1,128]{1,0:T(1,128)S(1)}, u32[]{:S(2)}, u32[]{:S(2)}) collective-permute-start(f32[1,128]{1,0:T(1,128)S(1)} %get-tuple-element.192), channel_id=1, source_target_pairs={{0,1},{1,2},{2,3},{3,4},{4,5},{5,6},{6,7},{7,0},{8,9},{9,10},{10,1... | collective-permute-start | bytes 1544 | tf_op jit(solution)/shard_map/ppermute | solution.py:16
  1.8 4.3 copy-start
  1.8 160.3 %collective-permute-start.1 = (f32[1,128]{1,0:T(1,128)S(1)}, f32[1,128]{1,0:T(1,128)S(1)}, u32[]{:S(2)}, u32[]{:S(2)}) collective-permute-start(f32[1,128]{1,0:T(1,128)S(1)} %get-tuple-element.191), channel_id=1, source_target_pairs={{1,0},{2,1},{3,2},{4,3},{5,4},{6,5},{7,6},{0,7},{9,8},{10,9},{11,1... | collective-permute-start | bytes 1544 | tf_op jit(solution)/shard_map/ppermute | solution.py:19
  4.8 164.4 %collective-permute-start.5 = (f32[128]{0:T(128)S(1)}, f32[128]{0:T(128)S(1)}, u32[]{:S(2)}, u32[]{:S(2)}) collective-permute-start(f32[128]{0:T(128)S(1)} %get-tuple-element.189), channel_id=1, source_target_pairs={{0,1},{1,2},{2,3},{3,4},{4,5},{5,6},{6,7},{8,9},{9,10},{10,11},{11... | collective-permute-start | bytes 1544 | tf_op jit(solution)/shard_map/ppermute | solution.py:33
  6.3 162.6 %collective-permute-start.3 = (f32[512]{0:T(512)S(1)}, f32[512]{0:T(512)S(1)}, u32[]{:S(2)}, u32[]{:S(2)}) collective-permute-start(f32[512]{0:T(512)S(1)} %slice_reduce_fusion), channel_id=1, source_target_pairs={{0,8},{8,16},{16,24},{24,32},{32,40},{40,48},{48,56},{56,64},{64,7... | collective-permute-start | bytes 6152 | tf_op jit(solution)/shard_map/ppermute | solution.py:27
  163.0 8.5 collective-permute-start.4
  165.9 8.3 collective-permute-start.2
  168.9 5.3 copy-start.1
  175.6 79.0 %collective-permute-start.6 = (f32[1,128]{1,0:T(1,128)S(1)}, f32[1,128]{1,0:T(1,128)S(1)}, u32[]{:S(2)}, u32[]{:S(2)}) collective-permute-start(f32[1,128]{1,0:T(1,128)S(1)} %get-tuple-element.188), channel_id=1, source_target_pairs={{0,1},{1,2},{2,3},{3,4},{4,5},{5,6},{6,7},{7,0},{8,9},{9,10},{10,1... | collective-permute-start | bytes 1544 | tf_op jit(solution)/shard_map/ppermute | solution.py:16
  175.6 78.9 %collective-permute-start.7 = (f32[1,128]{1,0:T(1,128)S(1)}, f32[1,128]{1,0:T(1,128)S(1)}, u32[]{:S(2)}, u32[]{:S(2)}) collective-permute-start(f32[1,128]{1,0:T(1,128)S(1)} %get-tuple-element.187), channel_id=1, source_target_pairs={{1,0},{2,1},{3,2},{4,3},{5,4},{6,5},{7,6},{0,7},{9,8},{10,9},{11,1... | collective-permute-start | bytes 1544 | tf_op jit(solution)/shard_map/ppermute | solution.py:19
  255.4 8.5 collective-permute-start.9
  257.4 8.3 collective-permute-start.8
  266.1 78.6 %collective-permute-start.10 = (f32[1,128]{1,0:T(1,128)S(1)}, f32[1,128]{1,0:T(1,128)S(1)}, u32[]{:S(2)}, u32[]{:S(2)}) collective-permute-start(f32[1,128]{1,0:T(1,128)S(1)} %get-tuple-element.186), channel_id=1, source_target_pairs={{0,1},{1,2},{2,3},{3,4},{4,5},{5,6},{6,7},{7,0},{8,9},{9,10},{10,1... | collective-permute-start | bytes 1544 | tf_op jit(solution)/shard_map/ppermute | solution.py:16
  266.1 78.6 %collective-permute-start.11 = (f32[1,128]{1,0:T(1,128)S(1)}, f32[1,128]{1,0:T(1,128)S(1)}, u32[]{:S(2)}, u32[]{:S(2)}) collective-permute-start(f32[1,128]{1,0:T(1,128)S(1)} %get-tuple-element.185), channel_id=1, source_target_pairs={{1,0},{2,1},{3,2},{4,3},{5,4},{6,5},{7,6},{0,7},{9,8},{10,9},{11,1... | collective-permute-start | bytes 1544 | tf_op jit(solution)/shard_map/ppermute | solution.py:19
  345.5 8.5 collective-permute-start.13
  348.5 8.3 collective-permute-start.12
  357.2 78.6 %collective-permute-start.14 = (f32[1,128]{1,0:T(1,128)S(1)}, f32[1,128]{1,0:T(1,128)S(1)}, u32[]{:S(2)}, u32[]{:S(2)}) collective-permute-start(f32[1,128]{1,0:T(1,128)S(1)} %get-tuple-element.184), channel_id=1, source_target_pairs={{0,1},{1,2},{2,3},{3,4},{4,5},{5,6},{6,7},{7,0},{8,9},{9,10},{10,1... | collective-permute-start | bytes 1544 | tf_op jit(solution)/shard_map/ppermute | solution.py:16
  357.2 78.6 %collective-permute-start.15 = (f32[1,128]{1,0:T(1,128)S(1)}, f32[1,128]{1,0:T(1,128)S(1)}, u32[]{:S(2)}, u32[]{:S(2)}) collective-permute-start(f32[1,128]{1,0:T(1,128)S(1)} %get-tuple-element.183), channel_id=1, source_target_pairs={{1,0},{2,1},{3,2},{4,3},{5,4},{6,5},{7,6},{0,7},{9,8},{10,9},{11,1... | collective-permute-start | bytes 1544 | tf_op jit(solution)/shard_map/ppermute | solution.py:19
  436.7 8.5 collective-permute-start.17
  438.7 8.5 collective-permute-start.16
  449.3 79.8 %collective-permute-start.18 = (f32[1,128]{1,0:T(1,128)S(1)}, f32[1,128]{1,0:T(1,128)S(1)}, u32[]{:S(2)}, u32[]{:S(2)}) collective-permute-start(f32[1,128]{1,0:T(1,128)S(1)} %get-tuple-element.182), channel_id=1, source_target_pairs={{0,1},{1,2},{2,3},{3,4},{4,5},{5,6},{6,7},{7,0},{8,9},{9,10},{10,1... | collective-permute-start | bytes 1544 | tf_op jit(solution)/shard_map/ppermute | solution.py:16
  449.3 79.8 %collective-permute-start.19 = (f32[1,128]{1,0:T(1,128)S(1)}, f32[1,128]{1,0:T(1,128)S(1)}, u32[]{:S(2)}, u32[]{:S(2)}) collective-permute-start(f32[1,128]{1,0:T(1,128)S(1)} %get-tuple-element.181), channel_id=1, source_target_pairs={{1,0},{2,1},{3,2},{4,3},{5,4},{6,5},{7,6},{0,7},{9,8},{10,9},{11,1... | collective-permute-start | bytes 1544 | tf_op jit(solution)/shard_map/ppermute | solution.py:19
  529.2 8.3 collective-permute-start.21
  532.2 8.4 collective-permute-start.20
  541.9 78.6 %collective-permute-start.22 = (f32[1,128]{1,0:T(1,128)S(1)}, f32[1,128]{1,0:T(1,128)S(1)}, u32[]{:S(2)}, u32[]{:S(2)}) collective-permute-start(f32[1,128]{1,0:T(1,128)S(1)} %get-tuple-element.180), channel_id=1, source_target_pairs={{0,1},{1,2},{2,3},{3,4},{4,5},{5,6},{6,7},{7,0},{8,9},{9,10},{10,1... | collective-permute-start | bytes 1544 | tf_op jit(solution)/shard_map/ppermute | solution.py:16
  542.0 78.6 %collective-permute-start.23 = (f32[1,128]{1,0:T(1,128)S(1)}, f32[1,128]{1,0:T(1,128)S(1)}, u32[]{:S(2)}, u32[]{:S(2)}) collective-permute-start(f32[1,128]{1,0:T(1,128)S(1)} %get-tuple-element.179), channel_id=1, source_target_pairs={{1,0},{2,1},{3,2},{4,3},{5,4},{6,5},{7,6},{0,7},{9,8},{10,9},{11,1... | collective-permute-start | bytes 1544 | tf_op jit(solution)/shard_map/ppermute | solution.py:19
  621.5 8.5 collective-permute-start.25
  623.4 8.7 collective-permute-start.24
  633.4 78.6 %collective-permute-start.26 = (f32[1,128]{1,0:T(1,128)S(1)}, f32[1,128]{1,0:T(1,128)S(1)}, u32[]{:S(2)}, u32[]{:S(2)}) collective-permute-start(f32[1,128]{1,0:T(1,128)S(1)} %get-tuple-element.178), channel_id=1, source_target_pairs={{0,1},{1,2},{2,3},{3,4},{4,5},{5,6},{6,7},{7,0},{8,9},{9,10},{10,1... | collective-permute-start | bytes 1544 | tf_op jit(solution)/shard_map/ppermute | solution.py:16
  633.5 78.6 %collective-permute-start.27 = (f32[1,128]{1,0:T(1,128)S(1)}, f32[1,128]{1,0:T(1,128)S(1)}, u32[]{:S(2)}, u32[]{:S(2)}) collective-permute-start(f32[1,128]{1,0:T(1,128)S(1)} %get-tuple-element.177), channel_id=1, source_target_pairs={{1,0},{2,1},{3,2},{4,3},{5,4},{6,5},{7,6},{0,7},{9,8},{10,9},{11,1... | collective-permute-start | bytes 1544 | tf_op jit(solution)/shard_map/ppermute | solution.py:19
  712.9 8.5 collective-permute-start.29
  715.9 8.6 collective-permute-start.28
  725.9 78.6 %collective-permute-start.30 = (f32[1,128]{1,0:T(1,128)S(1)}, f32[1,128]{1,0:T(1,128)S(1)}, u32[]{:S(2)}, u32[]{:S(2)}) collective-permute-start(f32[1,128]{1,0:T(1,128)S(1)} %get-tuple-element.176), channel_id=1, source_target_pairs={{0,1},{1,2},{2,3},{3,4},{4,5},{5,6},{6,7},{7,0},{8,9},{9,10},{10,1... | collective-permute-start | bytes 1544 | tf_op jit(solution)/shard_map/ppermute | solution.py:16
  725.9 78.6 %collective-permute-start.31 = (f32[1,128]{1,0:T(1,128)S(1)}, f32[1,128]{1,0:T(1,128)S(1)}, u32[]{:S(2)}, u32[]{:S(2)}) collective-permute-start(f32[1,128]{1,0:T(1,128)S(1)} %get-tuple-element.175), channel_id=1, source_target_pairs={{1,0},{2,1},{3,2},{4,3},{5,4},{6,5},{7,6},{0,7},{9,8},{10,9},{11,1... | collective-permute-start | bytes 1544 | tf_op jit(solution)/shard_map/ppermute | solution.py:19
  805.4 8.5 collective-permute-start.33
  807.3 8.3 collective-permute-start.32
  854.0 33.2 %all-to-all-start = ((f32[64,8,128]{2,1,0:T(8,128)}), f32[64,8,128]{2,1,0:T(8,128)S(1)}, u32[]{:S(2)}, u32[]{:S(2)}) async-start(f32[64,8,128]{2,1,0:T(8,128)} %constant_dynamic-update-slice_fusion), calls=%async_computation | async-start | bytes 524288 | tf_op jit(solution)/shard_map/all_to_all | solution.py:138
